TPU v7x, 32 devices: a whole 2x2x4 slice. The times are simulated.
32 devices in a mesh: seq: 8 (over z, y), mp: 4 (over x, core).
Axes of the slice: x: 2, y: 2, z: 4, core: 2. Of those that a mesh axis runs over, the one named last changes fastest.
Arguments:
- y_first: bfloat16 [2048, 896], P('seq', 'mp'), may hold values from -6 to 6
- y_second: bfloat16 [2048, 896], P('seq', 'mp'), may hold values from -10 to 10
- grad_first: bfloat16 [2048, 896], P('seq', 'mp'), may hold values from -6 to 6
- grad_second: bfloat16 [2048, 896], P('seq', 'mp'), may hold values from -6 to 6
- doc_blocks: int32 [12], replicated, may hold values from 1 to 2, as said below
- last_fill: int32 [12], replicated, may hold values from 1 to 128
- plan: int32 [16], replicated, may hold values from 0 to 15, as said below
- q_weight: bfloat16 [896, 512], P(None, 'mp'), may hold values from -1 to 1
- kv_weight: bfloat16 [2, 896, 128], P(None, 'mp'), may hold values from -1 to 1
- out_weight: bfloat16 [512, 896], P('mp'), may hold values from -0.25 to 0.25
- gate_up: bfloat16 [2, 896, 2560], P(None, None, 'mp'), may hold values from -0.1875 to 0.1875
- down_weight: bfloat16 [2560, 896], P('mp'), may hold values from -0.125 to 0.125
Outputs:
- first_input: bfloat16 [2048, 896], P('seq', 'mp')
- second_input: bfloat16 [2048, 896], P('seq', 'mp')
- first_grad: bfloat16 [2048, 896], P('seq', 'mp')
- second_grad: bfloat16 [2048, 896], P('seq', 'mp')
- q_weight_grad: float32 [896, 512], P('seq', 'mp')
- kv_weight_grad: float32 [2, 896, 128], P(None, 'seq')
- out_weight_grad: float32 [512, 896], P('mp', 'seq')
Inputs may be any that keep to these rules, and one draw needn't show every extreme that they name: `doc_blocks`: each document holds 1 or 2 blocks; together they fill all 16 blocks; exactly 4 documents hold 2. A permutation: block b goes to slot plan[b]; slots k * 2 to (k + 1) * 2 - 1 belong to index k of seq; the blocks of one document go to consecutive slots of one index, in order, the first at an even slot.
All inputs are finite; a program needn't handle non-finite values.
Results may differ from a plain program's by a relative error of at most 0.024.
Values may be sent and summed in bfloat16 or wider, within the bound.
A program may use at most 64 MiB of HBM per device.

v0:
```python
import math
import jax
import jax.numpy as jnp
from jax import lax
from jax.sharding import PartitionSpec as P

BLOCK = 128
EPSILON = 1e-06


def for_sending(value):
    return jax.tree.map(lambda a: a.astype(jnp.bfloat16) if a.dtype == jnp.float32 else a, value)


def normalize(values):
    inverse = lax.rsqrt(jnp.mean(values * values, axis=-1, keepdims=True) + EPSILON)
    return (values * inverse, inverse)


def block_table(doc_blocks, last_fill, block_count):
    doc_count = doc_blocks.shape[0]
    starts = jnp.cumsum(doc_blocks) - doc_blocks
    index = jnp.arange(block_count, dtype=jnp.int32)
    owner_doc = jnp.sum((starts[None, :] <= index[:, None]).astype(jnp.int32), axis=1) - 1
    onehot = (owner_doc[:, None] == jnp.arange(doc_count, dtype=jnp.int32)[None, :]).astype(
        jnp.int32
    )
    first_block = jnp.sum(onehot * starts[None, :], axis=1)
    length = jnp.sum(onehot * doc_blocks[None, :], axis=1)
    filled = jnp.sum(onehot * last_fill[None, :], axis=1)
    limit = jnp.where(index - first_block == length - 1, filled, BLOCK)
    return (owner_doc, limit)


def attend_mask(doc_rows, valid_rows):
    count = doc_rows.shape[-1]
    order = jnp.arange(count, dtype=jnp.int32)
    causal = order[None, :] <= order[:, None]
    same_doc = doc_rows[..., :, None] == doc_rows[..., None, :]
    keep = valid_rows[..., None, :] | (order[None, :] == order[:, None])
    return same_doc & causal & keep


def contract_last(left, right):
    return lax.dot_general(
        left, right, (((1,), (1,)), ((), ())), preferred_element_type=jnp.float32
    )


def contract_first(left, right):
    return lax.dot_general(
        left, right, (((0,), (0,)), ((), ())), preferred_element_type=jnp.float32
    )


def to_owners(streams, source):
    pieces = lax.axis_size("seq")
    row_total, feat_width = streams[0].shape
    slot_count = row_total // BLOCK
    share_rows = BLOCK // pieces
    split = tuple((item.reshape(slot_count, pieces, share_rows, feat_width) for item in streams))
    held = jax.tree.map(
        lambda part, own: part.astype(own.dtype),
        lax.all_to_all(for_sending(split), "seq", split_axis=1, concat_axis=0, tiled=True),
        split,
    )
    placed = tuple(
        (item[source].reshape(pieces, slot_count, share_rows, feat_width) for item in held)
    )
    owned = jax.tree.map(
        lambda part, own: part.astype(own.dtype),
        lax.all_to_all(for_sending(placed), "seq", split_axis=0, concat_axis=2, tiled=True),
        placed,
    )
    return tuple((item.reshape(row_total, feat_width) for item in owned))


def shards(
    y_first,
    y_second,
    grad_first,
    grad_second,
    doc_blocks,
    last_fill,
    plan,
    q_weight,
    kv_weight,
    out_weight,
    gate_up,
    down_weight,
):
    f32 = jnp.float32
    bf16 = jnp.bfloat16
    block_count = plan.shape[0]
    source = (
        jnp.zeros((block_count,), jnp.int32).at[plan].set(jnp.arange(block_count, dtype=jnp.int32))
    )
    owner_doc, limit = block_table(doc_blocks, last_fill, block_count)
    moved = to_owners((y_first, y_second, grad_first, grad_second), source)
    share_width = moved[0].shape[1]
    first, second, cot_first, cot_second, kv_full = (
        lax.all_gather(moved[0], "mp", axis=1, tiled=True),
        lax.all_gather(moved[1], "mp", axis=1, tiled=True),
        lax.all_gather(moved[2], "mp", axis=1, tiled=True),
        lax.all_gather(moved[3], "mp", axis=1, tiled=True),
        lax.all_gather(kv_weight, "mp", axis=1, tiled=True),
    )
    row_total, width = first.shape
    slot_count = row_total // BLOCK
    owned_slots = lax.axis_index("seq") * slot_count + jnp.arange(slot_count, dtype=jnp.int32)
    mine = source[owned_slots]
    row_doc = jnp.repeat(owner_doc[mine], BLOCK, total_repeat_length=row_total)
    row_limit = jnp.repeat(limit[mine], BLOCK, total_repeat_length=row_total)
    valid = jnp.arange(row_total, dtype=jnp.int32) % BLOCK < row_limit
    column_start = lax.axis_index("mp") * share_width

    def own_share(values):
        return lax.dynamic_slice_in_dim(values, column_start, share_width, 1)

    n_one, r_one = normalize(first.astype(f32))
    n_one_b = n_one.astype(bf16)
    gate_pre = jnp.dot(n_one_b, gate_up[0], preferred_element_type=f32)
    up_pre = jnp.dot(n_one_b, gate_up[1], preferred_element_type=f32)
    sigma = jax.nn.sigmoid(gate_pre)
    silu_gate = gate_pre * sigma
    hidden = (silu_gate * up_pre).astype(bf16)
    mix_part = jnp.dot(hidden, down_weight, preferred_element_type=f32)
    mixed = lax.psum(mix_part, "mp")
    second_in = (second.astype(f32) - mixed).astype(bf16)
    d_hidden = contract_last(cot_second, down_weight)
    d_gate = (d_hidden * up_pre * sigma * (1.0 + gate_pre * (1.0 - sigma))).astype(bf16)
    d_up = (d_hidden * silu_gate).astype(bf16)
    norm_part = contract_last(d_gate, gate_up[0]) + contract_last(d_up, gate_up[1])
    norm_share = lax.psum_scatter(
        norm_part.astype(jnp.bfloat16), "mp", scatter_dimension=1, tiled=True
    ).astype(jnp.float32)
    n_one_share = own_share(n_one)
    inner = lax.psum(jnp.sum(norm_share * n_one_share, axis=1, keepdims=True), "mp") / width
    first_share = (moved[2].astype(f32) + (norm_share - n_one_share * inner) * r_one).astype(bf16)
    first_cot = lax.all_gather(first_share, "mp", axis=1, tiled=True)
    kv_count = kv_full.shape[0]
    head_size = kv_full.shape[2] // 2
    local_heads = q_weight.shape[1] // head_size
    per_group = local_heads * lax.axis_size("mp") // kv_count
    group = lax.axis_index("mp") * local_heads // per_group
    kv_local = lax.dynamic_index_in_dim(kv_full, group, 0, keepdims=False)
    n_two, r_two = normalize(second_in.astype(f32))
    n_two_b = n_two.astype(bf16)
    query = jnp.dot(n_two_b, q_weight, preferred_element_type=f32).astype(bf16)
    keyval = jnp.dot(n_two_b, kv_local, preferred_element_type=f32).astype(bf16)
    pair_rows = 2 * BLOCK
    pair_count = row_total // pair_rows
    query_groups = query.reshape(pair_count, pair_rows, local_heads, head_size)
    key_groups = keyval[:, :head_size].reshape(pair_count, pair_rows, head_size)
    value_groups = keyval[:, head_size:].reshape(pair_count, pair_rows, head_size)
    allowed = attend_mask(
        row_doc.reshape(pair_count, pair_rows), valid.reshape(pair_count, pair_rows)
    )
    scale = 1.0 / math.sqrt(head_size)
    scores = (
        jnp.einsum("gihd,gjd->ghij", query_groups, key_groups, preferred_element_type=f32) * scale
    )
    scores = jnp.where(allowed[:, None], scores, -1e30)
    highest = jnp.max(scores, axis=-1, keepdims=True)
    expo = jnp.exp(scores - highest)
    probs = expo / jnp.sum(expo, axis=-1, keepdims=True)
    probs_b = probs.astype(bf16)
    heads_out = (
        jnp.einsum("ghij,gjd->gihd", probs_b, value_groups, preferred_element_type=f32)
        .astype(bf16)
        .reshape(row_total, local_heads * head_size)
    )
    attn = lax.psum(
        jnp.dot(heads_out, out_weight, preferred_element_type=f32).astype(jnp.bfloat16), "mp"
    ).astype(jnp.float32)
    live = valid[:, None]
    first_in = (first.astype(f32) - live.astype(f32) * attn).astype(bf16)
    masked_cot = first_cot * live.astype(bf16)
    out_grad = contract_first(heads_out, masked_cot)
    d_out = (
        contract_last(masked_cot, out_weight)
        .astype(bf16)
        .reshape(pair_count, pair_rows, local_heads, head_size)
    )
    d_prob = jnp.einsum("gihd,gjd->ghij", d_out, value_groups, preferred_element_type=f32)
    delta = jnp.sum(probs * d_prob, axis=-1, keepdims=True)
    d_score = (probs * (d_prob - delta) * scale).astype(bf16)
    d_query = (
        jnp.einsum("ghij,gjd->gihd", d_score, key_groups, preferred_element_type=f32)
        .astype(bf16)
        .reshape(row_total, local_heads * head_size)
    )
    d_key = jnp.einsum("ghij,gihd->gjhd", d_score, query_groups, preferred_element_type=f32).astype(
        bf16
    )
    d_value = jnp.einsum("ghij,gihd->gjhd", probs_b, d_out, preferred_element_type=f32).astype(bf16)
    q_grad = contract_first(n_two_b, d_query)
    norm_groups = n_two_b.reshape(pair_count, pair_rows, width)
    key_grad = jnp.einsum("gsk,gshd->kd", norm_groups, d_key, preferred_element_type=f32)
    value_grad = jnp.einsum("gsk,gshd->kd", norm_groups, d_value, preferred_element_type=f32)
    kv_own = jnp.concatenate([key_grad, value_grad], axis=1)
    d_norm_two = contract_last(d_query, q_weight)
    d_norm_two = d_norm_two + jnp.einsum(
        "gshd,kd->gsk", d_key, kv_local[:, :head_size], preferred_element_type=f32
    ).reshape(row_total, width)
    d_norm_two = d_norm_two + jnp.einsum(
        "gshd,kd->gsk", d_value, kv_local[:, head_size:], preferred_element_type=f32
    ).reshape(row_total, width)
    d_norm_two = lax.psum(d_norm_two.astype(jnp.bfloat16), "mp").astype(jnp.float32)
    inner_two = jnp.mean(d_norm_two * n_two, axis=-1, keepdims=True)
    second_cot = (cot_second.astype(f32) + (d_norm_two - n_two * inner_two) * r_two).astype(bf16)
    q_share = lax.psum_scatter(q_grad, "seq", scatter_dimension=0, tiled=True)
    kv_grad = jnp.zeros((kv_count, width, 2 * head_size), f32)
    kv_grad = lax.dynamic_update_index_in_dim(kv_grad, kv_own, group, 0)
    out_share, kv_part = (
        lax.psum_scatter(out_grad, "seq", scatter_dimension=1, tiled=True),
        lax.psum_scatter(kv_grad, "seq", scatter_dimension=1, tiled=True),
    )
    kv_share = lax.psum(kv_part, "mp")
    return (
        own_share(first_in),
        own_share(second_in),
        first_share,
        own_share(second_cot),
        q_share,
        kv_share,
        out_share,
    )


def solution(mesh):
    return jax.shard_map(
        shards,
        mesh=mesh,
        in_specs=(
            P("seq", "mp"),
            P("seq", "mp"),
            P("seq", "mp"),
            P("seq", "mp"),
            P(),
            P(),
            P(),
            P(None, "mp"),
            P(None, "mp", None),
            P("mp", None),
            P(None, None, "mp"),
            P("mp", None),
        ),
        out_specs=(
            P("seq", "mp"),
            P("seq", "mp"),
            P("seq", "mp"),
            P("seq", "mp"),
            P("seq", "mp"),
            P(None, "seq", None),
            P("mp", "seq"),
        ),
        check_vma=False,
    )
```

profile of v0, /device:TPU:0, one launch (start us, length us, event | category | flops | bytes accessed | tf_op | source)
XLA Modules:
  0.0 467.6 jit_solution(3869260832934583238)
XLA Ops:
  9.0 7.3 %all-to-all-start = ((bf16[2,8,16,224]{3,2,0,1:T(8,128)(2,1)}), bf16[2,8,16,224]{3,2,0,1:T(8,128)(2,1)S(1)}, u32[]{:S(2)}, u32[]{:S(2)}) async-start(bf16[2,8,16,224]{3,2,0,1:T(8,128)(2,1)} %copy.94), calls=%async_computation | async-start | bytes 262144 | tf_op jit(solution)/shard_map/all_to_all | solution.py:64
  23.6 5.5 %all-to-all-start.6 = ((bf16[2,8,16,224]{3,2,0,1:T(8,128)(2,1)}), bf16[2,8,16,224]{3,2,0,1:T(8,128)(2,1)S(1)}, u32[]{:S(2)}, u32[]{:S(2)}) async-start(bf16[2,8,16,224]{3,2,0,1:T(8,128)(2,1)} %copy.107), calls=%async_computation.6 | async-start | bytes 262144 | tf_op jit(solution)/shard_map/all_to_all | solution.py:64
  29.7 6.8 %all-to-all-done.6 = bf16[2,8,16,224]{3,2,0,1:T(8,128)(2,1)S(1)} async-done(((bf16[2,8,16,224]{3,2,0,1:T(8,128)(2,1)}), bf16[2,8,16,224]{3,2,0,1:T(8,128)(2,1)S(1)}, u32[]{:S(2)}, u32[]{:S(2)}) %all-to-all-start.6) | async-done | bytes 114720 | tf_op jit(solution)/shard_map/all_to_all | solution.py:64
  36.5 3.4 all-to-all-start.4
  42.0 6.8 %all_gather.17 = bf16[2,896,128]{2,1,0:T(8,128)(2,1)S(1)} all-gather(bf16[2,224,128]{2,1,0:T(8,128)(2,1)S(1)} %copy-done.16), channel_id=1, replica_groups=mesh['seq'=8,'mp'=4] {'mp'}, dimensions={1}, use_global_device_ids=true | all-gather | bytes 573440 | tf_op jit(solution)/shard_map/all_gather | solution.py:106
  48.8 5.9 %all-to-all-start.2 = ((bf16[2,8,16,224]{3,2,0,1:T(8,128)(2,1)}), bf16[2,8,16,224]{3,2,0,1:T(8,128)(2,1)S(1)}, u32[]{:S(2)}, u32[]{:S(2)}) async-start(bf16[2,8,16,224]{3,2,0,1:T(8,128)(2,1)} %copy.98), calls=%async_computation.2 | async-start | bytes 262144 | tf_op jit(solution)/shard_map/all_to_all | solution.py:64
  57.2 5.0 %all-to-all-done.2 = bf16[2,8,16,224]{3,2,0,1:T(8,128)(2,1)S(1)} async-done(((bf16[2,8,16,224]{3,2,0,1:T(8,128)(2,1)}), bf16[2,8,16,224]{3,2,0,1:T(8,128)(2,1)S(1)}, u32[]{:S(2)}, u32[]{:S(2)}) %all-to-all-start.2) | async-done | bytes 114720 | tf_op jit(solution)/shard_map/all_to_all | solution.py:64
  62.2 3.4 all-to-all-start.1
  76.4 6.3 %all_gather.15 = bf16[256,896]{0,1:T(8,128)(2,1)S(1)} all-gather(bf16[256,224]{0,1:T(8,128)(2,1)S(1)} %copy.96), channel_id=1, replica_groups=mesh['seq'=8,'mp'=4] {'mp'}, dimensions={1}, use_global_device_ids=true | all-gather | bytes 573440 | tf_op jit(solution)/shard_map/all_gather | solution.py:102
  87.1 5.9 %all-to-all-start.5 = ((bf16[8,2,16,224]{3,2,1,0:T(8,128)(2,1)}), bf16[8,2,16,224]{3,2,1,0:T(8,128)(2,1)S(1)}, u32[]{:S(2)}, u32[]{:S(2)}) async-start(bf16[8,2,16,224]{3,2,1,0:T(8,128)(2,1)} %bitcast.42), calls=%async_computation.5 | async-start | bytes 262144 | tf_op jit(solution)/shard_map/all_to_all | solution.py:72
  93.2 6.8 %all_gather.18 = bf16[256,896]{0,1:T(8,128)(2,1)S(1)} all-gather(bf16[256,224]{0,1:T(8,128)(2,1)S(1)} %copy.109), channel_id=1, replica_groups=mesh['seq'=8,'mp'=4] {'mp'}, dimensions={1}, use_global_device_ids=true | all-gather | bytes 573440 | tf_op jit(solution)/shard_map/all_gather | solution.py:105
  105.4 5.7 %all-to-all-start.3 = ((bf16[8,2,16,224]{3,2,1,0:T(8,128)(2,1)}), bf16[8,2,16,224]{3,2,1,0:T(8,128)(2,1)S(1)}, u32[]{:S(2)}, u32[]{:S(2)}) async-start(bf16[8,2,16,224]{3,2,1,0:T(8,128)(2,1)} %bitcast.20), calls=%async_computation.3 | async-start | bytes 262144 | tf_op jit(solution)/shard_map/all_to_all | solution.py:72
  112.9 5.7 %all-to-all-done.3 = bf16[8,2,16,224]{3,2,1,0:T(8,128)(2,1)S(1)} async-done(((bf16[8,2,16,224]{3,2,1,0:T(8,128)(2,1)}), bf16[8,2,16,224]{3,2,1,0:T(8,128)(2,1)S(1)}, u32[]{:S(2)}, u32[]{:S(2)}) %all-to-all-start.3) | async-done | bytes 114720 | tf_op jit(solution)/shard_map/all_to_all | solution.py:72
  118.7 8.9 %all_gather.16 = bf16[256,896]{0,1:T(8,128)(2,1)S(1)} all-gather(bf16[256,224]{0,1:T(8,128)(2,1)S(1)} %copy.100), channel_id=1, replica_groups=mesh['seq'=8,'mp'=4] {'mp'}, dimensions={1}, use_global_device_ids=true | all-gather | bytes 573440 | tf_op jit(solution)/shard_map/all_gather | solution.py:103
  127.8 3.4 fusion.1
  131.3 19.7 %all-reduce.5.cloned.1.call-done = f32[256,896]{1,0:T(8,128)} async-done(((f32[256,896]{1,0:T(8,128)}), f32[256,896]{1,0:T(8,128)}) %all-reduce.5.cloned.1.call-update) | async-done | bytes 917520 | tf_op jit(solution)/shard_map/psum | solution.py:128
  156.9 17.9 %reduce-scatter.5.cloned.1.call-done = bf16[256,224]{0,1:T(8,128)(2,1)} async-done(((bf16[256,896]{0,1:T(8,128)(2,1)}), bf16[256,224]{0,1:T(8,128)(2,1)}) %reduce-scatter.5.cloned.1.call-update) | async-done | bytes 114704 | tf_op jit(solution)/shard_map/reduce_scatter | solution.py:134
  175.9 5.8 %psum.37 = f32[256,1]{0,1:T(1,128)S(1)} all-reduce(f32[256,1]{0,1:T(1,128)S(1)} %bitcast.175), channel_id=1, replica_groups=mesh['seq'=8,'mp'=4] {'mp'}, use_global_device_ids=true, to_apply=%region_14.16 | all-reduce | flops 256 | bytes 2048 | tf_op jit(solution)/shard_map/psum | solution.py:138
  182.8 6.5 %all_gather.19 = bf16[256,896]{0,1:T(8,128)(2,1)S(1)} all-gather(bf16[256,224]{0,1:T(8,128)(2,1)S(1)} %fusion.40), channel_id=1, replica_groups=mesh['seq'=8,'mp'=4] {'mp'}, dimensions={1}, use_global_device_ids=true | all-gather | bytes 573440 | tf_op jit(solution)/shard_map/all_gather | solution.py:140
  202.1 27.5 %all-reduce.9.cloned.1.call-done = (bf16[256,896]{0,1:T(8,128)(2,1)}, bf16[256,896]{1,0:T(8,128)(2,1)}) async-done(((bf16[256,896]{0,1:T(8,128)(2,1)}, bf16[256,896]{1,0:T(8,128)(2,1)}), (bf16[256,896]{0,1:T(8,128)(2,1)}, bf16[256,896]{1,0:T(8,128)(2,1)})) %all-reduce.9.cloned.1.call-update) | async-done | bytes 917520 | tf_op jit(solution)/shard_map/psum | solution.py:173
  231.4 65.5 %reduce-scatter.9.cloned.1.call-done = f32[2,112,128]{2,1,0:T(8,128)} async-done(((f32[2,896,128]{2,1,0:T(8,128)}), f32[2,112,128]{2,1,0:T(8,128)}) %reduce-scatter.9.cloned.1.call-update) | async-done | bytes 114704 | tf_op jit(solution)/shard_map/reduce_scatter | solution.py:217
  299.3 62.8 %reduce-scatter.11.cloned.1.call-done = f32[128,112]{0,1:T(8,128)} async-done(((f32[128,896]{0,1:T(8,128)}), f32[128,112]{0,1:T(8,128)}) %reduce-scatter.11.cloned.1.call-update) | async-done | bytes 57360 | tf_op jit(solution)/shard_map/reduce_scatter | solution.py:216
  362.1 65.3 %reduce-scatter.7.cloned.1.call-done = f32[112,128]{1,0:T(8,128)} async-done(((f32[896,128]{1,0:T(8,128)}), f32[112,128]{1,0:T(8,128)}) %reduce-scatter.7.cloned.1.call-update) | async-done | bytes 57360 | tf_op jit(solution)/shard_map/reduce_scatter | solution.py:212
  427.4 31.8 %all-reduce.7.cloned.1.call-done = f32[2,112,128]{2,1,0:T(8,128)} async-done(((f32[2,112,128]{2,1,0:T(8,128)}), f32[2,112,128]{2,1,0:T(8,128)}) %all-reduce.7.cloned.1.call-update) | async-done | bytes 114704 | tf_op jit(solution)/shard_map/psum | solution.py:219
  (175 shorter events, 63.3 us)
Async XLA Ops:
  7.2 92.8 %copy-start = (bf16[640,896]{1,0:T(8,128)(2,1)S(1)}, bf16[640,896]{1,0:T(8,128)(2,1)}, u32[]{:S(2)}) copy-start(bf16[640,896]{1,0:T(8,128)(2,1)} %param.29) | copy-start | bytes 3440644
  7.2 11.4 %copy-start.14 = (bf16[256,224]{0,1:T(8,128)(2,1)S(1)}, bf16[256,224]{0,1:T(8,128)(2,1)}, u32[]{:S(2)}) copy-start(bf16[256,224]{0,1:T(8,128)(2,1)} %param.20) | copy-start | bytes 344068
  7.2 12.2 %copy-start.24 = (s32[12]{0:T(128)S(1)}, s32[12]{0:T(128)}, u32[]{:S(2)}) copy-start(s32[12]{0:T(128)} %param.22) | copy-start | bytes 148
  7.2 13.8 %copy-start.25 = (s32[12]{0:T(128)S(1)}, s32[12]{0:T(128)}, u32[]{:S(2)}) copy-start(s32[12]{0:T(128)} %param.23) | copy-start | bytes 148
  9.0 14.7 %all-to-all-start = ((bf16[2,8,16,224]{3,2,0,1:T(8,128)(2,1)}), bf16[2,8,16,224]{3,2,0,1:T(8,128)(2,1)S(1)}, u32[]{:S(2)}, u32[]{:S(2)}) async-start(bf16[2,8,16,224]{3,2,0,1:T(8,128)(2,1)} %copy.94), calls=%async_computation | async-start | bytes 262144 | tf_op jit(solution)/shard_map/all_to_all | solution.py:64
  19.4 21.8 %copy-start.15 = (bf16[256,224]{0,1:T(8,128)(2,1)S(1)}, bf16[256,224]{0,1:T(8,128)(2,1)}, u32[]{:S(2)}) copy-start(bf16[256,224]{0,1:T(8,128)(2,1)} %param.19) | copy-start | bytes 344068
  21.0 21.0 %copy-start.16 = (bf16[2,224,128]{2,1,0:T(8,128)(2,1)S(1)}, bf16[2,224,128]{2,1,0:T(8,128)(2,1)}, u32[]{:S(2)}) copy-start(bf16[2,224,128]{2,1,0:T(8,128)(2,1)} %param.26) | copy-start | bytes 344068
  23.6 12.8 %all-to-all-start.6 = ((bf16[2,8,16,224]{3,2,0,1:T(8,128)(2,1)}), bf16[2,8,16,224]{3,2,0,1:T(8,128)(2,1)S(1)}, u32[]{:S(2)}, u32[]{:S(2)}) async-start(bf16[2,8,16,224]{3,2,0,1:T(8,128)(2,1)} %copy.107), calls=%async_computation.6 | async-start | bytes 262144 | tf_op jit(solution)/shard_map/all_to_all | solution.py:64
  36.5 12.3 %all-to-all-start.4 = ((bf16[2,8,16,224]{3,2,0,1:T(8,128)(2,1)}), bf16[2,8,16,224]{3,2,0,1:T(8,128)(2,1)S(1)}, u32[]{:S(2)}, u32[]{:S(2)}) async-start(bf16[2,8,16,224]{3,2,0,1:T(8,128)(2,1)} %copy.104), calls=%async_computation.4 | async-start | bytes 262144 | tf_op jit(solution)/shard_map/all_to_all | solution.py:64
  41.1 24.4 %copy-start.22 = (pred[256]{0:T(512)(128)(4,1)}, pred[256]{0:T(512)(128)(4,1)S(1)}, u32[]{:S(2)}) copy-start(pred[256]{0:T(512)(128)(4,1)S(1)} %get-tuple-element.69) | copy-start | bytes 772
  48.8 13.4 %all-to-all-start.2 = ((bf16[2,8,16,224]{3,2,0,1:T(8,128)(2,1)}), bf16[2,8,16,224]{3,2,0,1:T(8,128)(2,1)S(1)}, u32[]{:S(2)}, u32[]{:S(2)}) async-start(bf16[2,8,16,224]{3,2,0,1:T(8,128)(2,1)} %copy.98), calls=%async_computation.2 | async-start | bytes 262144 | tf_op jit(solution)/shard_map/all_to_all | solution.py:64
  62.2 10.7 %all-to-all-start.1 = ((bf16[8,2,16,224]{3,2,1,0:T(8,128)(2,1)}), bf16[8,2,16,224]{3,2,1,0:T(8,128)(2,1)S(1)}, u32[]{:S(2)}, u32[]{:S(2)}) async-start(bf16[8,2,16,224]{3,2,1,0:T(8,128)(2,1)} %bitcast.4), calls=%async_computation.1 | async-start | bytes 262144 | tf_op jit(solution)/shard_map/all_to_all | solution.py:72
  72.8 14.3 %all-to-all-start.7 = ((bf16[8,2,16,224]{3,2,1,0:T(8,128)(2,1)}), bf16[8,2,16,224]{3,2,1,0:T(8,128)(2,1)S(1)}, u32[]{:S(2)}, u32[]{:S(2)}) async-start(bf16[8,2,16,224]{3,2,1,0:T(8,128)(2,1)} %bitcast.50), calls=%async_computation.7 | async-start | bytes 262144 | tf_op jit(solution)/shard_map/all_to_all | solution.py:72
  87.1 18.2 %all-to-all-start.5 = ((bf16[8,2,16,224]{3,2,1,0:T(8,128)(2,1)}), bf16[8,2,16,224]{3,2,1,0:T(8,128)(2,1)S(1)}, u32[]{:S(2)}, u32[]{:S(2)}) async-start(bf16[8,2,16,224]{3,2,1,0:T(8,128)(2,1)} %bitcast.42), calls=%async_computation.5 | async-start | bytes 262144 | tf_op jit(solution)/shard_map/all_to_all | solution.py:72
  105.4 13.2 %all-to-all-start.3 = ((bf16[8,2,16,224]{3,2,1,0:T(8,128)(2,1)}), bf16[8,2,16,224]{3,2,1,0:T(8,128)(2,1)S(1)}, u32[]{:S(2)}, u32[]{:S(2)}) async-start(bf16[8,2,16,224]{3,2,1,0:T(8,128)(2,1)} %bitcast.20), calls=%async_computation.3 | async-start | bytes 262144 | tf_op jit(solution)/shard_map/all_to_all | solution.py:72
  111.1 39.9 %all-reduce.5.cloned.1.call-start = ((), (), s32[]{:S(2)}) async-start(), calls=%async_computation.12 | async-start | bytes 1835008 | tf_op jit(solution)/shard_map/psum | solution.py:128
  111.8 63.0 %reduce-scatter.5.cloned.1.call-start = ((), (), s32[]{:S(2)}) async-start(), calls=%async_computation.13 | async-start | bytes 573440 | tf_op jit(solution)/shard_map/reduce_scatter | solution.py:134
  131.2 98.4 %all-reduce.9.cloned.1.call-start = ((), (), s32[]{:S(2)}) async-start(), calls=%async_computation.18 | async-start | bytes 1835008 | tf_op jit(solution)/shard_map/psum | solution.py:173
  181.7 7.6 %copy-start.13 = (bf16[128,896]{1,0:T(8,128)(2,1)S(1)}, bf16[128,896]{1,0:T(8,128)(2,1)}, u32[]{:S(2)}) copy-start(bf16[128,896]{1,0:T(8,128)(2,1)} %param.27) | copy-start | bytes 688132
  181.7 7.9 %copy-start.21 = (bf16[256,128]{0,1:T(8,128)(2,1)S(1)}, bf16[256,128]{0,1:T(8,128)(2,1)}, u32[]{:S(2)}) copy-start(bf16[256,128]{0,1:T(8,128)(2,1)} %copy-done.20) | copy-start | bytes 196612
  193.4 103.5 %reduce-scatter.9.cloned.1.call-start = ((), (), s32[]{:S(2)}) async-start(), calls=%async_computation.15 | async-start | bytes 1032192 | tf_op jit(solution)/shard_map/reduce_scatter | solution.py:217
  196.8 165.3 %reduce-scatter.11.cloned.1.call-start = ((), (), s32[]{:S(2)}) async-start(), calls=%async_computation.17 | async-start | bytes 516096 | tf_op jit(solution)/shard_map/reduce_scatter | solution.py:216
  199.0 228.4 %reduce-scatter.7.cloned.1.call-start = ((), (), s32[]{:S(2)}) async-start(), calls=%async_computation.14 | async-start | bytes 516096 | tf_op jit(solution)/shard_map/reduce_scatter | solution.py:212
  201.0 258.1 %all-reduce.7.cloned.1.call-start = ((), (), s32[]{:S(2)}) async-start(), calls=%async_computation.16 | async-start | bytes 229376 | tf_op jit(solution)/shard_map/psum | solution.py:219
  (21 other events, 47.2 us)
Sparse Core Ops, SparseCore 0:
  114.3 36.6 all-reduce.4
  153.5 21.3 reduce-scatter.4
  193.5 36.0 all-reduce.8
  232.8 64.0 reduce-scatter.8
  300.6 61.4 reduce-scatter.10
  365.8 61.5 reduce-scatter.6
  429.7 29.4 all-reduce.6
where the time goes:
time: 469 us; the launch traced here: 468 us
  waiting for transfers between devices  312 us (67%)
  blocking collectives  41 us (9%)
  starting transfers between devices  40.8 us (9%)
  matrix products  23.1 us (5%)
  local copies, waits for them, and re-layouts  22.9 us (5%)
  between operations  14.8 us (3%)
  other arithmetic  13 us (3%)
    reduce_scatter x1, waiting for transfers between devices, shards(): lax.psum_scatter(kv_grad, 'seq', scatter_dimension=1, tiled=True)  65.5 us
    reduce_scatter x1, waiting for transfers between devices, shards(): q_share = lax.psum_scatter(q_grad, 'seq', scatter_dimension=0, tiled=True)  65.3 us
    reduce_scatter x1, waiting for transfers between devices, shards(): lax.psum_scatter(out_grad, 'seq', scatter_dimension=1, tiled=True)  62.8 us
    psum x1, waiting for transfers between devices, shards(): kv_share = lax.psum(kv_part, 'mp')  31.8 us
    psum x1, waiting for transfers between devices, shards(): lax.psum(jnp.dot(heads_out, out_weight, preferred_element_type=f32).astyp...  27.5 us
    all_to_all x4, starting transfers between devices, to_owners(): lax.all_to_all(for_sending(split), 'seq', split_axis=1, concat_axis=0, ti...  22.1 us
    psum x1, waiting for transfers between devices, shards(): mixed = lax.psum(mix_part, 'mp')  19.7 us
    all_to_all x4, starting transfers between devices, to_owners(): lax.all_to_all(for_sending(placed), 'seq', split_axis=0, concat_axis=2, t...  18.4 us
  transfers between devices with their start and end apart: 15, of which 12 were waited for; matrix products, arithmetic and copies ran while one was open for 10% of the time, Pallas kernels for 0%

commit v1 on v0

--- a/solution.py
+++ b/solution.py
@@ -216,7 +216,7 @@
         lax.psum_scatter(out_grad, "seq", scatter_dimension=1, tiled=True),
         lax.psum_scatter(kv_grad, "seq", scatter_dimension=1, tiled=True),
     )
-    kv_share = lax.psum(kv_part, "mp")
+    kv_share = jnp.sum(lax.all_gather(kv_part, "mp"), axis=0)
     return (
         own_share(first_in),
         own_share(second_in),

time: 469 us -> 449 us (0.957)
  waiting for transfers between devices: 312 us -> 274 us
  local copies, waits for them, and re-layouts: 22.9 us -> 32.3 us
  blocking collectives: 41 us -> 47.8 us
    unnamed x7, waiting for transfers between devices: 0.6 us -> 76.9 us
    reduce_scatter x1 -> x0, waiting for transfers between devices: 65.5 us -> none  [shards(): lax.psum_scatter(kv_grad, 'seq', scatter_dimension=1, tiled=True)]
    psum x1 -> x0, waiting for transfers between devices: 31.8 us -> none  [shards(): kv_share = lax.psum(kv_part, 'mp')]
    psum x1, waiting for transfers between devices: 27.5 us -> 16.4 us  [shards(): lax.psum(jnp.dot(heads_out, out_weight, preferred_element_type=f32).astyp...]
    dynamic_update_slice x1, local copies, waits for them, and re-layouts: 0.03 us -> 10.8 us  [shards(): kv_grad = lax.dynamic_update_index_in_dim(kv_grad, kv_own, group, 0)]
    all_gather x0 -> x1, blocking collectives: none -> 6.79 us  [shards(): kv_share = jnp.sum(lax.all_gather(kv_part, 'mp'), axis=0)]
    reduce_scatter x1, waiting for transfers between devices: 62.8 us -> 56.7 us  [shards(): lax.psum_scatter(out_grad, 'seq', scatter_dimension=1, tiled=True)]
    unnamed x68 -> x59, local copies, waits for them, and re-layouts: 9.81 us -> 8.12 us
  transfers between devices with their start and end apart: 15 -> 14, of which waited for: 12 -> 11; matrix products, arithmetic and copies ran while one was open for 10% -> 13% of each run, Pallas kernels for 0% -> 0%
where the time goes in v1:
time: 449 us; the launch traced here: 447 us
  waiting for transfers between devices  274 us (61%)
  blocking collectives  47.8 us (11%)
  starting transfers between devices  40.9 us (9%)
  local copies, waits for them, and re-layouts  32.3 us (7%)
  matrix products  23.1 us (5%)
  between operations  15.4 us (3%)
  other arithmetic  13.6 us (3%)
    unnamed x7, waiting for transfers between devices  76.9 us
    reduce_scatter x1, waiting for transfers between devices, shards(): q_share = lax.psum_scatter(q_grad, 'seq', scatter_dimension=0, tiled=True)  65.3 us
    reduce_scatter x1, waiting for transfers between devices, shards(): lax.psum_scatter(out_grad, 'seq', scatter_dimension=1, tiled=True)  56.7 us
    all_to_all x4, starting transfers between devices, to_owners(): lax.all_to_all(for_sending(split), 'seq', split_axis=1, concat_axis=0, ti...  22.1 us
    psum x1, waiting for transfers between devices, shards(): mixed = lax.psum(mix_part, 'mp')  19.7 us
    all_to_all x4, starting transfers between devices, to_owners(): lax.all_to_all(for_sending(placed), 'seq', split_axis=0, concat_axis=2, t...  18.4 us
    reduce_scatter x1, waiting for transfers between devices, shards(): lax.psum_scatter(norm_part.astype(jnp.bfloat16), 'mp', scatter_dimension=...  17.9 us
    psum x1, waiting for transfers between devices, shards(): lax.psum(jnp.dot(heads_out, out_weight, preferred_element_type=f32).astyp...  16.4 us
  transfers between devices with their start and end apart: 14, of which 11 were waited for; matrix products, arithmetic and copies ran while one was open for 13% of the time, Pallas kernels for 0%

profile of v1, /device:TPU:0, one launch (start us, length us, event | category | flops | bytes accessed | tf_op | source)
XLA Modules:
  0.0 446.9 jit_solution(10006467370226616929)
XLA Ops:
  9.0 7.3 %all-to-all-start = ((bf16[2,8,16,224]{3,2,0,1:T(8,128)(2,1)}), bf16[2,8,16,224]{3,2,0,1:T(8,128)(2,1)S(1)}, u32[]{:S(2)}, u32[]{:S(2)}) async-start(bf16[2,8,16,224]{3,2,0,1:T(8,128)(2,1)} %copy.98), calls=%async_computation | async-start | bytes 262144 | tf_op jit(solution)/shard_map/all_to_all | solution.py:64
  23.6 5.5 %all-to-all-start.6 = ((bf16[2,8,16,224]{3,2,0,1:T(8,128)(2,1)}), bf16[2,8,16,224]{3,2,0,1:T(8,128)(2,1)S(1)}, u32[]{:S(2)}, u32[]{:S(2)}) async-start(bf16[2,8,16,224]{3,2,0,1:T(8,128)(2,1)} %copy.111), calls=%async_computation.6 | async-start | bytes 262144 | tf_op jit(solution)/shard_map/all_to_all | solution.py:64
  29.7 6.8 %all-to-all-done.6 = bf16[2,8,16,224]{3,2,0,1:T(8,128)(2,1)S(1)} async-done(((bf16[2,8,16,224]{3,2,0,1:T(8,128)(2,1)}), bf16[2,8,16,224]{3,2,0,1:T(8,128)(2,1)S(1)}, u32[]{:S(2)}, u32[]{:S(2)}) %all-to-all-start.6) | async-done | bytes 114720 | tf_op jit(solution)/shard_map/all_to_all | solution.py:64
  36.5 3.4 all-to-all-start.4
  41.9 6.8 %all_gather.23 = bf16[2,896,128]{2,1,0:T(8,128)(2,1)S(1)} all-gather(bf16[2,224,128]{2,1,0:T(8,128)(2,1)S(1)} %copy-done.12), channel_id=1, replica_groups=mesh['seq'=8,'mp'=4] {'mp'}, dimensions={1}, use_global_device_ids=true | all-gather | bytes 573440 | tf_op jit(solution)/shard_map/all_gather | solution.py:106
  48.7 5.9 %all-to-all-start.2 = ((bf16[2,8,16,224]{3,2,0,1:T(8,128)(2,1)}), bf16[2,8,16,224]{3,2,0,1:T(8,128)(2,1)S(1)}, u32[]{:S(2)}, u32[]{:S(2)}) async-start(bf16[2,8,16,224]{3,2,0,1:T(8,128)(2,1)} %copy.102), calls=%async_computation.2 | async-start | bytes 262144 | tf_op jit(solution)/shard_map/all_to_all | solution.py:64
  57.2 5.0 %all-to-all-done.2 = bf16[2,8,16,224]{3,2,0,1:T(8,128)(2,1)S(1)} async-done(((bf16[2,8,16,224]{3,2,0,1:T(8,128)(2,1)}), bf16[2,8,16,224]{3,2,0,1:T(8,128)(2,1)S(1)}, u32[]{:S(2)}, u32[]{:S(2)}) %all-to-all-start.2) | async-done | bytes 114720 | tf_op jit(solution)/shard_map/all_to_all | solution.py:64
  76.3 6.3 %all_gather.21 = bf16[256,896]{0,1:T(8,128)(2,1)S(1)} all-gather(bf16[256,224]{0,1:T(8,128)(2,1)S(1)} %copy.100), channel_id=1, replica_groups=mesh['seq'=8,'mp'=4] {'mp'}, dimensions={1}, use_global_device_ids=true | all-gather | bytes 573440 | tf_op jit(solution)/shard_map/all_gather | solution.py:102
  87.1 5.9 %all-to-all-start.5 = ((bf16[8,2,16,224]{3,2,1,0:T(8,128)(2,1)}), bf16[8,2,16,224]{3,2,1,0:T(8,128)(2,1)S(1)}, u32[]{:S(2)}, u32[]{:S(2)}) async-start(bf16[8,2,16,224]{3,2,1,0:T(8,128)(2,1)} %bitcast.42), calls=%async_computation.5 | async-start | bytes 262144 | tf_op jit(solution)/shard_map/all_to_all | solution.py:72
  93.1 6.8 %all_gather.24 = bf16[256,896]{0,1:T(8,128)(2,1)S(1)} all-gather(bf16[256,224]{0,1:T(8,128)(2,1)S(1)} %copy.113), channel_id=1, replica_groups=mesh['seq'=8,'mp'=4] {'mp'}, dimensions={1}, use_global_device_ids=true | all-gather | bytes 573440 | tf_op jit(solution)/shard_map/all_gather | solution.py:105
  105.3 5.7 %all-to-all-start.3 = ((bf16[8,2,16,224]{3,2,1,0:T(8,128)(2,1)}), bf16[8,2,16,224]{3,2,1,0:T(8,128)(2,1)S(1)}, u32[]{:S(2)}, u32[]{:S(2)}) async-start(bf16[8,2,16,224]{3,2,1,0:T(8,128)(2,1)} %bitcast.20), calls=%async_computation.3 | async-start | bytes 262144 | tf_op jit(solution)/shard_map/all_to_all | solution.py:72
  112.8 5.7 %all-to-all-done.3 = bf16[8,2,16,224]{3,2,1,0:T(8,128)(2,1)S(1)} async-done(((bf16[8,2,16,224]{3,2,1,0:T(8,128)(2,1)}), bf16[8,2,16,224]{3,2,1,0:T(8,128)(2,1)S(1)}, u32[]{:S(2)}, u32[]{:S(2)}) %all-to-all-start.3) | async-done | bytes 114720 | tf_op jit(solution)/shard_map/all_to_all | solution.py:72
  118.6 8.9 %all_gather.22 = bf16[256,896]{0,1:T(8,128)(2,1)S(1)} all-gather(bf16[256,224]{0,1:T(8,128)(2,1)S(1)} %copy.104), channel_id=1, replica_groups=mesh['seq'=8,'mp'=4] {'mp'}, dimensions={1}, use_global_device_ids=true | all-gather | bytes 573440 | tf_op jit(solution)/shard_map/all_gather | solution.py:103
  127.7 3.4 fusion.1
  131.2 19.7 %all-reduce.6.cloned.1.call-done = f32[256,896]{1,0:T(8,128)} async-done(((f32[256,896]{1,0:T(8,128)}), f32[256,896]{1,0:T(8,128)}) %all-reduce.6.cloned.1.call-update) | async-done | bytes 917520 | tf_op jit(solution)/shard_map/psum | solution.py:128
  156.8 17.9 %reduce-scatter.4.cloned.1.call-done = bf16[256,224]{0,1:T(8,128)(2,1)} async-done(((bf16[256,896]{0,1:T(8,128)(2,1)}), bf16[256,224]{0,1:T(8,128)(2,1)}) %reduce-scatter.4.cloned.1.call-update) | async-done | bytes 114704 | tf_op jit(solution)/shard_map/reduce_scatter | solution.py:134
  175.8 5.8 %psum.30 = f32[256,1]{0,1:T(1,128)S(1)} all-reduce(f32[256,1]{0,1:T(1,128)S(1)} %bitcast.178), channel_id=1, replica_groups=mesh['seq'=8,'mp'=4] {'mp'}, use_global_device_ids=true, to_apply=%region_14.16 | all-reduce | flops 256 | bytes 2048 | tf_op jit(solution)/shard_map/psum | solution.py:138
  182.7 6.5 %all_gather.25 = bf16[256,896]{0,1:T(8,128)(2,1)S(1)} all-gather(bf16[256,224]{0,1:T(8,128)(2,1)S(1)} %fusion.40), channel_id=1, replica_groups=mesh['seq'=8,'mp'=4] {'mp'}, dimensions={1}, use_global_device_ids=true | all-gather | bytes 573440 | tf_op jit(solution)/shard_map/all_gather | solution.py:140
  195.2 10.8 %dynamic_update_slice.4 = f32[2,896,128]{2,0,1:T(2,128)S(1)} dynamic-update-slice(f32[2,896,128]{2,0,1:T(2,128)S(1)} %broadcast_in_dim.35, f32[1,896,128]{2,0,1:T(1,128)} %copy.119, s32[]{:T(128)S(6)} %select_n.78, s32[]{:T(128)} %constant.148.clone.1, s32[]{:T(128)} %constant.148.clone.1) | dynamic-update-slice | bytes 917508 | tf_op jit(solution)/shard_map/jit(dynamic_update_index_in_dim)/dynamic_update_slice | solution.py:214
  212.8 16.4 %all-reduce.10.cloned.1.call-done = (bf16[256,896]{0,1:T(8,128)(2,1)}, bf16[256,896]{1,0:T(8,128)(2,1)}) async-done(((bf16[256,896]{0,1:T(8,128)(2,1)}, bf16[256,896]{1,0:T(8,128)(2,1)}), (bf16[256,896]{0,1:T(8,128)(2,1)}, bf16[256,896]{1,0:T(8,128)(2,1)})) %all-reduce.10.cloned.1.call-update) | async-done | bytes 917520 | tf_op jit(solution)/shard_map/psum | solution.py:173
  233.3 76.4 %all-reduce.8.cloned.1.call-done = f32[2,896,128]{2,0,1:T(2,128)} async-done(((f32[2,896,128]{2,0,1:T(2,128)}), f32[2,896,128]{2,0,1:T(2,128)}) %all-reduce.8.cloned.1.call-update) | async-done | bytes 917520
  310.6 6.8 %all-gather = f32[8,112,128]{2,1,0:T(8,128)S(1)} all-gather(f32[2,112,128]{2,1,0:T(8,128)S(1)} %copy.120), channel_id=2, replica_groups=mesh['seq'=8,'mp'=4] {'mp'}, dimensions={0}, use_global_device_ids=true | all-gather | bytes 573440 | tf_op jit(solution)/shard_map/all_gather | solution.py:219
  318.1 56.7 %reduce-scatter.8.cloned.1.call-done = f32[128,112]{0,1:T(8,128)} async-done(((f32[128,896]{0,1:T(8,128)}), f32[128,112]{0,1:T(8,128)}) %reduce-scatter.8.cloned.1.call-update) | async-done | bytes 57360 | tf_op jit(solution)/shard_map/reduce_scatter | solution.py:216
  374.8 65.3 %reduce-scatter.6.cloned.1.call-done = f32[112,128]{1,0:T(8,128)} async-done(((f32[896,128]{1,0:T(8,128)}), f32[112,128]{1,0:T(8,128)}) %reduce-scatter.6.cloned.1.call-update) | async-done | bytes 57360 | tf_op jit(solution)/shard_map/reduce_scatter | solution.py:212
  (166 shorter events, 65.9 us)
Async XLA Ops:
  7.2 92.7 %copy-start = (bf16[640,896]{1,0:T(8,128)(2,1)S(1)}, bf16[640,896]{1,0:T(8,128)(2,1)}, u32[]{:S(2)}) copy-start(bf16[640,896]{1,0:T(8,128)(2,1)} %param.29) | copy-start | bytes 3440644
  7.2 11.4 %copy-start.10 = (bf16[256,224]{0,1:T(8,128)(2,1)S(1)}, bf16[256,224]{0,1:T(8,128)(2,1)}, u32[]{:S(2)}) copy-start(bf16[256,224]{0,1:T(8,128)(2,1)} %param.20) | copy-start | bytes 344068
  7.2 12.2 %copy-start.18 = (s32[12]{0:T(128)S(1)}, s32[12]{0:T(128)}, u32[]{:S(2)}) copy-start(s32[12]{0:T(128)} %param.22) | copy-start | bytes 148
  7.2 13.8 %copy-start.19 = (s32[12]{0:T(128)S(1)}, s32[12]{0:T(128)}, u32[]{:S(2)}) copy-start(s32[12]{0:T(128)} %param.23) | copy-start | bytes 148
  9.0 14.7 %all-to-all-start = ((bf16[2,8,16,224]{3,2,0,1:T(8,128)(2,1)}), bf16[2,8,16,224]{3,2,0,1:T(8,128)(2,1)S(1)}, u32[]{:S(2)}, u32[]{:S(2)}) async-start(bf16[2,8,16,224]{3,2,0,1:T(8,128)(2,1)} %copy.98), calls=%async_computation | async-start | bytes 262144 | tf_op jit(solution)/shard_map/all_to_all | solution.py:64
  19.4 21.8 %copy-start.11 = (bf16[256,224]{0,1:T(8,128)(2,1)S(1)}, bf16[256,224]{0,1:T(8,128)(2,1)}, u32[]{:S(2)}) copy-start(bf16[256,224]{0,1:T(8,128)(2,1)} %param.19) | copy-start | bytes 344068
  21.0 21.0 %copy-start.12 = (bf16[2,224,128]{2,1,0:T(8,128)(2,1)S(1)}, bf16[2,224,128]{2,1,0:T(8,128)(2,1)}, u32[]{:S(2)}) copy-start(bf16[2,224,128]{2,1,0:T(8,128)(2,1)} %param.26) | copy-start | bytes 344068
  23.6 12.8 %all-to-all-start.6 = ((bf16[2,8,16,224]{3,2,0,1:T(8,128)(2,1)}), bf16[2,8,16,224]{3,2,0,1:T(8,128)(2,1)S(1)}, u32[]{:S(2)}, u32[]{:S(2)}) async-start(bf16[2,8,16,224]{3,2,0,1:T(8,128)(2,1)} %copy.111), calls=%async_computation.6 | async-start | bytes 262144 | tf_op jit(solution)/shard_map/all_to_all | solution.py:64
  36.5 12.3 %all-to-all-start.4 = ((bf16[2,8,16,224]{3,2,0,1:T(8,128)(2,1)}), bf16[2,8,16,224]{3,2,0,1:T(8,128)(2,1)S(1)}, u32[]{:S(2)}, u32[]{:S(2)}) async-start(bf16[2,8,16,224]{3,2,0,1:T(8,128)(2,1)} %copy.108), calls=%async_computation.4 | async-start | bytes 262144 | tf_op jit(solution)/shard_map/all_to_all | solution.py:64
  48.7 13.4 %all-to-all-start.2 = ((bf16[2,8,16,224]{3,2,0,1:T(8,128)(2,1)}), bf16[2,8,16,224]{3,2,0,1:T(8,128)(2,1)S(1)}, u32[]{:S(2)}, u32[]{:S(2)}) async-start(bf16[2,8,16,224]{3,2,0,1:T(8,128)(2,1)} %copy.102), calls=%async_computation.2 | async-start | bytes 262144 | tf_op jit(solution)/shard_map/all_to_all | solution.py:64
  62.2 10.7 %all-to-all-start.1 = ((bf16[8,2,16,224]{3,2,1,0:T(8,128)(2,1)}), bf16[8,2,16,224]{3,2,1,0:T(8,128)(2,1)S(1)}, u32[]{:S(2)}, u32[]{:S(2)}) async-start(bf16[8,2,16,224]{3,2,1,0:T(8,128)(2,1)} %bitcast.4), calls=%async_computation.1 | async-start | bytes 262144 | tf_op jit(solution)/shard_map/all_to_all | solution.py:72
  72.8 14.3 %all-to-all-start.7 = ((bf16[8,2,16,224]{3,2,1,0:T(8,128)(2,1)}), bf16[8,2,16,224]{3,2,1,0:T(8,128)(2,1)S(1)}, u32[]{:S(2)}, u32[]{:S(2)}) async-start(bf16[8,2,16,224]{3,2,1,0:T(8,128)(2,1)} %bitcast.50), calls=%async_computation.7 | async-start | bytes 262144 | tf_op jit(solution)/shard_map/all_to_all | solution.py:72
  87.1 18.2 %all-to-all-start.5 = ((bf16[8,2,16,224]{3,2,1,0:T(8,128)(2,1)}), bf16[8,2,16,224]{3,2,1,0:T(8,128)(2,1)S(1)}, u32[]{:S(2)}, u32[]{:S(2)}) async-start(bf16[8,2,16,224]{3,2,1,0:T(8,128)(2,1)} %bitcast.42), calls=%async_computation.5 | async-start | bytes 262144 | tf_op jit(solution)/shard_map/all_to_all | solution.py:72
  93.1 7.4 %copy-start.21 = (bf16[2,896,640]{2,1,0:T(8,128)(2,1)S(1)}, bf16[2,896,640]{2,1,0:T(8,128)(2,1)}, u32[]{:S(2)}) copy-start(bf16[2,896,640]{2,1,0:T(8,128)(2,1)} %param.28) | copy-start | bytes 6881284
  105.3 13.2 %all-to-all-start.3 = ((bf16[8,2,16,224]{3,2,1,0:T(8,128)(2,1)}), bf16[8,2,16,224]{3,2,1,0:T(8,128)(2,1)S(1)}, u32[]{:S(2)}, u32[]{:S(2)}) async-start(bf16[8,2,16,224]{3,2,1,0:T(8,128)(2,1)} %bitcast.20), calls=%async_computation.3 | async-start | bytes 262144 | tf_op jit(solution)/shard_map/all_to_all | solution.py:72
  111.0 39.8 %all-reduce.6.cloned.1.call-start = ((), (), s32[]{:S(2)}) async-start(), calls=%async_computation.11 | async-start | bytes 1835008 | tf_op jit(solution)/shard_map/psum | solution.py:128
  111.7 63.0 %reduce-scatter.4.cloned.1.call-start = ((), (), s32[]{:S(2)}) async-start(), calls=%async_computation.12 | async-start | bytes 573440 | tf_op jit(solution)/shard_map/reduce_scatter | solution.py:134
  131.1 98.1 %all-reduce.10.cloned.1.call-start = ((), (), s32[]{:S(2)}) async-start(), calls=%async_computation.16 | async-start | bytes 1835008 | tf_op jit(solution)/shard_map/psum | solution.py:173
  181.5 7.6 %copy-start.9 = (bf16[128,896]{1,0:T(8,128)(2,1)S(1)}, bf16[128,896]{1,0:T(8,128)(2,1)}, u32[]{:S(2)}) copy-start(bf16[128,896]{1,0:T(8,128)(2,1)} %param.27) | copy-start | bytes 688132
  181.5 7.9 %copy-start.17 = (bf16[256,128]{0,1:T(8,128)(2,1)S(1)}, bf16[256,128]{0,1:T(8,128)(2,1)}, u32[]{:S(2)}) copy-start(bf16[256,128]{0,1:T(8,128)(2,1)} %copy-done.16) | copy-start | bytes 196612
  182.7 7.0 %copy-start.5 = (bf16[256,224]{0,1:T(8,128)(2,1)}, bf16[256,224]{0,1:T(8,128)(2,1)S(1)}, u32[]{:S(2)}) copy-start(bf16[256,224]{0,1:T(8,128)(2,1)S(1)} %fusion.40) | copy-start | bytes 344068
  193.0 116.7 %all-reduce.8.cloned.1.call-start = ((), (), s32[]{:S(2)}) async-start(), calls=%async_computation.15 | async-start | bytes 1835008
  207.0 167.8 %reduce-scatter.8.cloned.1.call-start = ((), (), s32[]{:S(2)}) async-start(), calls=%async_computation.14 | async-start | bytes 516096 | tf_op jit(solution)/shard_map/reduce_scatter | solution.py:216
  209.1 230.9 %reduce-scatter.6.cloned.1.call-start = ((), (), s32[]{:S(2)}) async-start(), calls=%async_computation.13 | async-start | bytes 516096 | tf_op jit(solution)/shard_map/reduce_scatter | solution.py:212
  (15 other events, 27.2 us)
Sparse Core Ops, SparseCore 0:
  114.2 36.5 all-reduce.5
  153.4 21.3 reduce-scatter.3
  193.1 36.0 all-reduce.9
  232.5 77.0 all-reduce.7
  313.4 61.3 reduce-scatter.7
  378.5 61.5 reduce-scatter.5
